TPU v7x, 256 devices: a whole 4x4x8 slice. The times are simulated.
256 devices in a mesh: dp: 4 (over x), seq: 16 (over z, core), tensor: 4 (over y).
Axes of the slice: x: 4, y: 4, z: 8, core: 2. Of those that a mesh axis runs over, the one named last changes fastest.
Arguments:
- feature_in: bfloat16 [16, 2048, 512], P('dp', 'seq', 'tensor'), may hold values from -6 to 6
- conv_weight: bfloat16 [2, 512, 512], P(None, 'tensor'), may hold values from -0.1875 to 0.1875
- proj_weight: bfloat16 [512, 1920], P(None, 'tensor'), may hold values from -0.25 to 0.25
- mask_embed: bfloat16 [1920], P('tensor'), may hold values from -5 to 5
- pos_weight: bfloat16 [128, 16, 120, 120], P(('dp', 'seq'), 'tensor'), may hold values from -0.046875 to 0.046875
- final_weight: bfloat16 [1920, 1024], P('tensor'), may hold values from -0.125 to 0.125
- codebook: bfloat16 [2, 320, 512], replicated, may hold values from -6 to 6
- quant_weight: bfloat16 [1024, 1024], replicated, may hold values from -0.1875 to 0.1875
- mask_starts: int32 [16, 66], P('dp'), may hold values from 0 to 1014
- code_choice: int32 [16, 1024, 2], P(('dp', 'tensor'), 'seq'), may hold values from 0 to 319
- negative_ids: int32 [16, 1024, 100], P(('dp', 'tensor'), 'seq'), may hold values from 0 to 1023, as said below
Outputs:
- frame_loss: float32 [16, 1024], P(('dp', 'tensor'), 'seq')
Inputs may be any that keep to these rules, and one draw needn't show every extreme that they name: `negative_ids`: each entry names a frame of the same utterance other than the frame itself.
All inputs are finite; a program needn't handle non-finite values.
Results may differ from a plain program's by a relative error of at most 0.00065.
Values may be sent and summed in bfloat16 or wider, within the bound.
A program may use at most 128 MiB of HBM per device.

v0:
```python
import jax
import jax.numpy as jnp
from jax import lax
from jax.sharding import PartitionSpec as P

KERNEL = 128
MASK_LEN = 10
ln_eps = 1e-05
norm_eps = 1e-06
logit_temp = 0.1


def extended(block, sides, width):
    for axis, dim in sides:
        count = lax.axis_size(axis)
        forward = [(i, i + 1) for i in range(count - 1)]
        backward = [(target, source) for source, target in forward]
        low = lax.ppermute(
            lax.slice_in_dim(block, block.shape[dim] - width, None, axis=dim), axis, forward
        )
        high = lax.ppermute(lax.slice_in_dim(block, 0, width, axis=dim), axis, backward)
        block = jnp.concatenate([low, block, high], axis=dim)
    return block


def make_targets(code_block, codebook, quant_weight):
    entries = codebook.shape[1]
    choices_row = jnp.arange(entries, dtype=jnp.int32)
    pieces = []
    for qgroup in range(codebook.shape[0]):
        onehot = (code_block[..., qgroup, None] == choices_row).astype(jnp.bfloat16)
        pieces.append(
            jnp.dot(onehot, codebook[qgroup], preferred_element_type=jnp.float32).astype(
                jnp.bfloat16
            )
        )
    codevec = jnp.concatenate(pieces, axis=-1)
    return jnp.dot(codevec, quant_weight, preferred_element_type=jnp.float32).astype(jnp.bfloat16)


def utterance_loss(context, own_targets, all_targets, neg_ids, is_masked):
    scores = jnp.einsum("fc,nc->fn", context, all_targets, preferred_element_type=jnp.float32)
    ctx_norm = jnp.einsum("fc,fc->f", context, context, preferred_element_type=jnp.float32)
    own_norm = jnp.einsum("fc,fc->f", own_targets, own_targets, preferred_element_type=jnp.float32)
    tgt_norm = jnp.einsum("nc,nc->n", all_targets, all_targets, preferred_element_type=jnp.float32)
    pos_dot = jnp.einsum("fc,fc->f", context, own_targets, preferred_element_type=jnp.float32)
    neg_dot = jnp.take_along_axis(scores, neg_ids, axis=1)
    neg_norm = tgt_norm[neg_ids]
    positive = pos_dot * lax.rsqrt((ctx_norm + norm_eps) * (own_norm + norm_eps)) / logit_temp
    negative = (
        neg_dot * lax.rsqrt((ctx_norm[:, None] + norm_eps) * (neg_norm + norm_eps)) / logit_temp
    )
    frame_loss = jnp.log(jnp.exp(positive) + jnp.sum(jnp.exp(negative), axis=-1)) - positive
    return jnp.where(is_masked, frame_loss, jnp.zeros_like(frame_loss))


def tap_sum(windows, running, tap_block, frames):
    count = tap_block.shape[0]
    joined_taps = max((d for d in range(1, 17) if count % d == 0))
    group_count, inner, outer = (tap_block.shape[1], tap_block.shape[2], tap_block.shape[3])

    def add_block(step, partial_value):
        base = step * joined_taps
        slabs = [
            lax.dynamic_slice_in_dim(windows, base + offset, frames, 1)
            for offset in range(joined_taps)
        ]
        joined = jnp.concatenate(slabs, axis=-1)
        taps = lax.dynamic_slice_in_dim(tap_block, base, joined_taps, 0)
        taps = jnp.transpose(taps, (1, 0, 2, 3)).reshape(group_count, joined_taps * inner, outer)
        return partial_value + jnp.einsum(
            "ufgi,gio->ufgo", joined, taps, preferred_element_type=jnp.float32
        )

    return lax.fori_loop(0, count // joined_taps, add_block, running)


def on_device(
    feature_in,
    conv_weight,
    proj_weight,
    mask_embed,
    pos_weight,
    final_weight,
    codebook,
    quant_weight,
    mask_starts,
    code_choice,
    negative_ids,
):
    utt_count, sample_rows, channels = feature_in.shape
    frames = sample_rows // 2
    frame_pairs = feature_in.reshape(utt_count, frames, 2 * channels)
    conv_term = jnp.dot(
        frame_pairs,
        conv_weight.reshape(2 * channels, conv_weight.shape[2]),
        preferred_element_type=jnp.float32,
    )
    summed = lax.psum(conv_term, "tensor")
    row_mean = jnp.mean(summed, axis=-1, keepdims=True)
    row_square = jnp.mean(summed * summed, axis=-1, keepdims=True)
    normed = (summed - row_mean) * lax.rsqrt(row_square - row_mean * row_mean + ln_eps)
    features = jax.nn.gelu(normed, approximate=False).astype(jnp.bfloat16)
    projected = jnp.dot(features, proj_weight, preferred_element_type=jnp.float32).astype(
        jnp.bfloat16
    )
    positions = (lax.axis_index("seq") * frames + jnp.arange(frames, dtype=jnp.int32))[
        None, :, None
    ]
    starts = mask_starts[:, None, :]
    masked = jnp.any((positions >= starts) & (positions < starts + MASK_LEN), axis=-1)
    hidden = jnp.where(masked[..., None], mask_embed[None, None, :], projected)
    padded = extended(hidden, (("seq", 1),), KERNEL // 2)
    group_count = pos_weight.shape[1]
    inner = pos_weight.shape[2]
    outer = pos_weight.shape[3]
    windows = padded.reshape(utt_count, padded.shape[1], group_count, inner)
    initial = jnp.zeros((utt_count, frames, group_count, outer), jnp.float32)
    conv_out = tap_sum(
        windows, initial, lax.all_gather(pos_weight, ("dp", "seq"), axis=0, tiled=True), frames
    )
    conv_out = conv_out.reshape(utt_count, frames, group_count * outer)
    mixed = (hidden.astype(jnp.float32) + jax.nn.gelu(conv_out, approximate=False)).astype(
        jnp.bfloat16
    )
    utt_rows = utt_count // lax.axis_size("tensor")
    context = lax.psum_scatter(
        jnp.dot(mixed, final_weight, preferred_element_type=jnp.float32),
        "tensor",
        scatter_dimension=0,
        tiled=True,
    ).astype(jnp.bfloat16)
    own_targets = make_targets(code_choice, codebook, quant_weight)
    all_targets = lax.all_gather(own_targets, "seq", axis=1, tiled=True)
    is_masked = lax.dynamic_slice_in_dim(masked, lax.axis_index("tensor") * utt_rows, utt_rows, 0)
    return jax.vmap(utterance_loss)(context, own_targets, all_targets, negative_ids, is_masked)


def solution(mesh):
    return jax.shard_map(
        on_device,
        mesh=mesh,
        in_specs=(
            P("dp", "seq", "tensor"),
            P(None, "tensor", None),
            P(None, "tensor"),
            P("tensor"),
            P(("dp", "seq"), "tensor", None, None),
            P("tensor", None),
            P(),
            P(),
            P("dp", None),
            P(("dp", "tensor"), "seq", None),
            P(("dp", "tensor"), "seq", None),
        ),
        out_specs=P(("dp", "tensor"), "seq"),
        check_vma=False,
    )
```

profile of v0, /device:TPU:1, one launch (start us, length us, event | category | flops | bytes accessed | tf_op | source)
XLA Modules:
  0.0 506.4 jit_solution(2708013920155017598)
XLA Ops:
  12.7 48.5 %all-reduce.2.cloned.1.call-done = f32[4,64,512]{2,1,0:T(8,128)} async-done(((f32[4,64,512]{2,1,0:T(8,128)}), f32[4,64,512]{2,1,0:T(8,128)}) %all-reduce.2.cloned.1.call-update) | async-done | bytes 524304 | tf_op jit(solution)/shard_map/psum | solution.py:99
  65.0 5.1 %collective-permute-start = (bf16[4,64,480]{2,1,0:T(8,128)(2,1)S(1)}, bf16[4,64,480]{2,1,0:T(8,128)(2,1)S(1)}, u32[]{:S(2)}, u32[]{:S(2)}) collective-permute-start(bf16[4,64,480]{2,1,0:T(8,128)(2,1)S(1)} %fusion.1), channel_id=1, source_target_pairs={{0,4},{4,8},{8,12},{12,16},{16,20},{20,24},{24,28},{28,32},{32,36}... | collective-permute-start | bytes 737288 | tf_op jit(solution)/shard_map/ppermute | solution.py:18
  72.0 6.7 %collective-permute-done = bf16[4,64,480]{2,1,0:T(8,128)(2,1)S(1)} collective-permute-done((bf16[4,64,480]{2,1,0:T(8,128)(2,1)S(1)}, bf16[4,64,480]{2,1,0:T(8,128)(2,1)S(1)}, u32[]{:S(2)}, u32[]{:S(2)}) %collective-permute-start) | collective-permute-done | bytes 245792 | tf_op jit(solution)/shard_map/ppermute | solution.py:18
  78.8 4.0 collective-permute-done.1
  86.5 28.4 %all-gather.4.cloned.1.call-done = bf16[128,4,120,120]{3,2,1,0:T(8,128)(2,1)} async-done(((bf16[2,4,120,120]{3,2,1,0:T(8,128)(2,1)}), bf16[128,4,120,120]{3,2,1,0:T(8,128)(2,1)}) %all-gather.4.cloned.1.call-update) | async-done | bytes 14745616 | tf_op jit(solution)/shard_map/all_gather | solution.py:120
  114.9 222.5 %while.16 = (s32[]{:T(128)}, f32[4,64,4,120]{3,1,0,2:T(8,128)}, bf16[128,4,120,120]{3,2,1,0:T(8,128)(2,1)}, bf16[4,192,4,120]{3,1,0,2:T(8,128)(2,1)S(1)}, s32[]{...) while((s32[]{:T(128)}, f32[4,64,4,120]{3,1,0,2:T(8,128)}, ...), condition=%wide.region_5.6_spmd.clone, body=%wide.region_4.5_spmd.clone.sunk | while | flops 472105024 | bytes 34530440 | solution.py:75
  117.9 7.1 %concatenate.26 = bf16[4,64,4,1920]{3,1,0,2:T(8,128)(2,1)} concatenate(bf16[4,64,4,120]{3,1,0,2:T(8,128)(2,1)} %get-tuple-element.238, bf16[4,64,4,120]{3,1,0,2:T(8,128)(2,1)} %get-tuple-element.239, bf16[4,64,4,120]{3,1,0,2:T(8,128)(2,1)} %get-tuple-element.240, bf16[4,64,4,120]{3,1,0,2:T(8,128)(2,1)} %get-tuple-element.241, bf16[4,64,4,120]{3,1,0,2:T(8,128)(2,1)} %get-tuple-element.242, ...), dimensions={3} | concatenate | bytes 7864320 | tf_op jit(solution)/shard_map/while/body/eval_jaxpr/concatenate | solution.py:68
  128.0 4.4 copy.47
  132.5 4.6 reshape.312
  137.1 3.8 fusion.188
  144.8 7.1 %concatenate.26 = bf16[4,64,4,1920]{3,1,0,2:T(8,128)(2,1)} concatenate(bf16[4,64,4,120]{3,1,0,2:T(8,128)(2,1)} %get-tuple-element.238, bf16[4,64,4,120]{3,1,0,2:T(8,128)(2,1)} %get-tuple-element.239, bf16[4,64,4,120]{3,1,0,2:T(8,128)(2,1)} %get-tuple-element.240, bf16[4,64,4,120]{3,1,0,2:T(8,128)(2,1)} %get-tuple-element.241, bf16[4,64,4,120]{3,1,0,2:T(8,128)(2,1)} %get-tuple-element.242, ...), dimensions={3} | concatenate | bytes 7864320 | tf_op jit(solution)/shard_map/while/body/eval_jaxpr/concatenate | solution.py:68
  151.9 3.0 constant_dynamic-slice_fusion.19
  154.9 4.4 copy.47
  159.4 4.6 reshape.312
  164.0 3.8 fusion.188
  172.7 7.1 %concatenate.26 = bf16[4,64,4,1920]{3,1,0,2:T(8,128)(2,1)} concatenate(bf16[4,64,4,120]{3,1,0,2:T(8,128)(2,1)} %get-tuple-element.238, bf16[4,64,4,120]{3,1,0,2:T(8,128)(2,1)} %get-tuple-element.239, bf16[4,64,4,120]{3,1,0,2:T(8,128)(2,1)} %get-tuple-element.240, bf16[4,64,4,120]{3,1,0,2:T(8,128)(2,1)} %get-tuple-element.241, bf16[4,64,4,120]{3,1,0,2:T(8,128)(2,1)} %get-tuple-element.242, ...), dimensions={3} | concatenate | bytes 7864320 | tf_op jit(solution)/shard_map/while/body/eval_jaxpr/concatenate | solution.py:68
  182.9 4.4 copy.47
  187.3 4.6 reshape.312
  191.9 3.8 fusion.188
  200.7 7.1 %concatenate.26 = bf16[4,64,4,1920]{3,1,0,2:T(8,128)(2,1)} concatenate(bf16[4,64,4,120]{3,1,0,2:T(8,128)(2,1)} %get-tuple-element.238, bf16[4,64,4,120]{3,1,0,2:T(8,128)(2,1)} %get-tuple-element.239, bf16[4,64,4,120]{3,1,0,2:T(8,128)(2,1)} %get-tuple-element.240, bf16[4,64,4,120]{3,1,0,2:T(8,128)(2,1)} %get-tuple-element.241, bf16[4,64,4,120]{3,1,0,2:T(8,128)(2,1)} %get-tuple-element.242, ...), dimensions={3} | concatenate | bytes 7864320 | tf_op jit(solution)/shard_map/while/body/eval_jaxpr/concatenate | solution.py:68
  207.8 3.0 constant_dynamic-slice_fusion.19
  210.9 4.4 copy.47
  215.3 4.6 reshape.312
  219.9 3.8 fusion.188
  228.6 7.1 %concatenate.26 = bf16[4,64,4,1920]{3,1,0,2:T(8,128)(2,1)} concatenate(bf16[4,64,4,120]{3,1,0,2:T(8,128)(2,1)} %get-tuple-element.238, bf16[4,64,4,120]{3,1,0,2:T(8,128)(2,1)} %get-tuple-element.239, bf16[4,64,4,120]{3,1,0,2:T(8,128)(2,1)} %get-tuple-element.240, bf16[4,64,4,120]{3,1,0,2:T(8,128)(2,1)} %get-tuple-element.241, bf16[4,64,4,120]{3,1,0,2:T(8,128)(2,1)} %get-tuple-element.242, ...), dimensions={3} | concatenate | bytes 7864320 | tf_op jit(solution)/shard_map/while/body/eval_jaxpr/concatenate | solution.py:68
  238.8 4.4 copy.47
  243.2 4.6 reshape.312
  247.8 3.8 fusion.188
  256.5 7.1 %concatenate.26 = bf16[4,64,4,1920]{3,1,0,2:T(8,128)(2,1)} concatenate(bf16[4,64,4,120]{3,1,0,2:T(8,128)(2,1)} %get-tuple-element.238, bf16[4,64,4,120]{3,1,0,2:T(8,128)(2,1)} %get-tuple-element.239, bf16[4,64,4,120]{3,1,0,2:T(8,128)(2,1)} %get-tuple-element.240, bf16[4,64,4,120]{3,1,0,2:T(8,128)(2,1)} %get-tuple-element.241, bf16[4,64,4,120]{3,1,0,2:T(8,128)(2,1)} %get-tuple-element.242, ...), dimensions={3} | concatenate | bytes 7864320 | tf_op jit(solution)/shard_map/while/body/eval_jaxpr/concatenate | solution.py:68
  263.7 3.0 constant_dynamic-slice_fusion.19
  266.7 4.4 copy.47
  271.2 4.6 reshape.312
  275.7 3.8 fusion.188
  284.5 7.1 %concatenate.26 = bf16[4,64,4,1920]{3,1,0,2:T(8,128)(2,1)} concatenate(bf16[4,64,4,120]{3,1,0,2:T(8,128)(2,1)} %get-tuple-element.238, bf16[4,64,4,120]{3,1,0,2:T(8,128)(2,1)} %get-tuple-element.239, bf16[4,64,4,120]{3,1,0,2:T(8,128)(2,1)} %get-tuple-element.240, bf16[4,64,4,120]{3,1,0,2:T(8,128)(2,1)} %get-tuple-element.241, bf16[4,64,4,120]{3,1,0,2:T(8,128)(2,1)} %get-tuple-element.242, ...), dimensions={3} | concatenate | bytes 7864320 | tf_op jit(solution)/shard_map/while/body/eval_jaxpr/concatenate | solution.py:68
  291.6 3.0 constant_dynamic-slice_fusion.19
  294.7 4.4 copy.47
  299.1 4.6 reshape.312
  303.7 3.9 fusion.188
  312.5 7.1 %concatenate.26 = bf16[4,64,4,1920]{3,1,0,2:T(8,128)(2,1)} concatenate(bf16[4,64,4,120]{3,1,0,2:T(8,128)(2,1)} %get-tuple-element.238, bf16[4,64,4,120]{3,1,0,2:T(8,128)(2,1)} %get-tuple-element.239, bf16[4,64,4,120]{3,1,0,2:T(8,128)(2,1)} %get-tuple-element.240, bf16[4,64,4,120]{3,1,0,2:T(8,128)(2,1)} %get-tuple-element.241, bf16[4,64,4,120]{3,1,0,2:T(8,128)(2,1)} %get-tuple-element.242, ...), dimensions={3} | concatenate | bytes 7864320 | tf_op jit(solution)/shard_map/while/body/eval_jaxpr/concatenate | solution.py:68
  319.6 3.0 constant_dynamic-slice_fusion.19
  322.7 4.4 copy.47
  327.1 4.6 reshape.312
  331.7 3.8 fusion.188
  340.7 3.8 fusion.4
  347.1 19.4 %reduce-scatter.2.cloned.1.call-done = f32[1,64,1024]{2,1,0:T(8,128)} async-done(((f32[4,64,1024]{2,1,0:T(8,128)}), f32[1,64,1024]{2,1,0:T(8,128)}) %reduce-scatter.2.cloned.1.call-update) | async-done | bytes 262160 | tf_op jit(solution)/shard_map/reduce_scatter | solution.py:127
  369.3 41.1 %all-gather.6.cloned.1.call-done = bf16[1024,1024]{1,0:T(8,128)(2,1)} async-done(((bf16[64,1024]{1,0:T(8,128)(2,1)}), bf16[1024,1024]{1,0:T(8,128)(2,1)}) %all-gather.6.cloned.1.call-update) | async-done | bytes 2097168 | tf_op jit(solution)/shard_map/all_gather | solution.py:134
  412.7 48.5 %gather_fusion = f32[6400]{0:T(1024)S(1)} fusion(f32[1,64,1024]{2,1,0:T(8,128)S(1)} %convolution_bitcast_fusion, s32[6400]{0:T(1024)S(1)} %reshape.273), kind=kCustom, calls=%fused_computation | custom fusion | bytes 128000 | tf_op jit(solution)/shard_map/vmap(jit(take_along_axis))/gather | solution.py:47
  463.3 35.1 %gather_fusion.1 = f32[6400]{0:T(1024)S(1)} fusion(f32[1,1024]{1,0:T(1,128)S(1)} %bitcast.82, s32[6400]{0:T(1024)S(1)} %reshape.281), kind=kCustom, calls=%fused_computation.1 | custom fusion | bytes 102400 | tf_op jit(solution)/shard_map/vmap()/gather | solution.py:48
  (78 shorter events, 75.8 us)
Async XLA Ops:
  7.4 359.2 %copy-start = (bf16[1024,1024]{1,0:T(8,128)(2,1)S(1)}, bf16[1024,1024]{1,0:T(8,128)(2,1)}, u32[]{:S(2)}) copy-start(bf16[1024,1024]{1,0:T(8,128)(2,1)} %param.20) | copy-start | bytes 6291460
  7.4 53.8 %all-reduce.2.cloned.1.call-start = ((), (), s32[]{:S(2)}) async-start(), calls=%async_computation.1 | async-start | bytes 1048576 | tf_op jit(solution)/shard_map/psum | solution.py:99
  10.5 104.4 %all-gather.4.cloned.1.call-start = ((), (), s32[]{:S(2)}) async-start(), calls=%async_computation.2 | async-start | bytes 15974400 | tf_op jit(solution)/shard_map/all_gather | solution.py:120
  11.1 355.5 %reduce-scatter.2.cloned.1.call-start = ((), (), s32[]{:S(2)}) async-start(), calls=%async_computation.3 | async-start | bytes 1310720 | tf_op jit(solution)/shard_map/reduce_scatter | solution.py:127
  65.0 49.9 %copy-start.2 = (bf16[4,64,480]{2,1,0:T(8,128)(2,1)}, bf16[4,64,480]{2,1,0:T(8,128)(2,1)S(1)}, u32[]{:S(2)}) copy-start(bf16[4,64,480]{2,1,0:T(8,128)(2,1)S(1)} %fusion.1) | copy-start | bytes 737284
  65.0 13.7 %collective-permute-start = (bf16[4,64,480]{2,1,0:T(8,128)(2,1)S(1)}, bf16[4,64,480]{2,1,0:T(8,128)(2,1)S(1)}, u32[]{:S(2)}, u32[]{:S(2)}) collective-permute-start(bf16[4,64,480]{2,1,0:T(8,128)(2,1)S(1)} %fusion.1), channel_id=1, source_target_pairs={{0,4},{4,8},{8,12},{12,16},{16,20},{20,24},{24,28},{28,32},{32,36}... | collective-permute-start | bytes 737288 | tf_op jit(solution)/shard_map/ppermute | solution.py:18
  70.1 12.7 %collective-permute-start.1 = (bf16[4,64,480]{2,1,0:T(8,128)(2,1)S(1)}, bf16[4,64,480]{2,1,0:T(8,128)(2,1)}, u32[]{:S(2)}, u32[]{:S(2)}) collective-permute-start(bf16[4,64,480]{2,1,0:T(8,128)(2,1)S(1)} %fusion.1), channel_id=1, source_target_pairs={{4,0},{8,4},{12,8},{16,12},{20,16},{24,20},{28,24},{32,28},{36,32}... | collective-permute-start | bytes 737288 | tf_op jit(solution)/shard_map/ppermute | solution.py:21
  337.5 3.2 copy-start.3
  340.7 4.1 copy-start.5
  344.5 24.4 %copy-start.4 = (s32[1,64,100]{2,1,0:T(8,128)S(1)}, s32[1,64,100]{2,1,0:T(8,128)}, u32[]{:S(2)}) copy-start(s32[1,64,100]{2,1,0:T(8,128)} %param.23) | copy-start | bytes 76804
  344.5 65.8 %all-gather.6.cloned.1.call-start = ((), (), s32[]{:S(2)}) async-start(), calls=%async_computation.4 | async-start | bytes 2228224 | tf_op jit(solution)/shard_map/all_gather | solution.py:134
  366.5 43.8 %copy-start.1 = (f32[1,64,1024]{2,1,0:T(8,128)S(1)}, f32[1,64,1024]{2,1,0:T(8,128)}, u32[]{:S(2)}) copy-start(f32[1,64,1024]{2,1,0:T(8,128)} %reduce-scatter.2.cloned.1.call-done) | copy-start | bytes 786436
Sparse Core Ops, SparseCore 0:
  10.6 50.5 all-reduce.1
  344.6 21.8 reduce-scatter.1
  369.0 41.2 all-gather.5
Sparse Core Ops, SparseCore 1:
  13.7 101.2 all-gather.3
where the time goes:
time: 514 us; the launch traced here: 506 us
  local copies, waits for them, and re-layouts  267 us (52%)
  waiting for transfers between devices  149 us (29%)
  matrix products  46.2 us (9%)
  other arithmetic  22.3 us (4%)
  between operations  14.8 us (3%)
  starting transfers between devices  7.3 us (1%)
    dynamic_slice x16, local copies, waits for them, and re-layouts, add_block(): taps = lax.dynamic_slice_in_dim(tap_block, base, joined_taps, 0)  59.7 us
    concatenate x8, local copies, waits for them, and re-layouts, add_block(): joined = jnp.concatenate(slabs, axis=-1)  57.2 us
    gather x4, local copies, waits for them, and re-layouts, utterance_loss(): neg_dot = jnp.take_along_axis(scores, neg_ids, axis=1)  48.7 us
    psum x1, waiting for transfers between devices, on_device(): summed = lax.psum(conv_term, 'tensor')  48.5 us
    all_gather x1, waiting for transfers between devices, on_device(): all_targets = lax.all_gather(own_targets, 'seq', axis=1, tiled=True)  41.1 us
    reshape x8, local copies, waits for them, and re-layouts, add_block(): jnp.transpose(taps, (1, 0, 2, 3))  36.6 us
    gather x3, local copies, waits for them, and re-layouts, utterance_loss(): neg_norm = tgt_norm[neg_ids]  35.2 us
    while x8, matrix products  30.8 us
  transfers between devices with their start and end apart: 6, of which 6 were waited for; matrix products, arithmetic and copies ran while one was open for 2% of the time, Pallas kernels for 0%

commit v1 on v0

--- a/solution.py
+++ b/solution.py
@@ -8,6 +8,14 @@
 ln_eps = 1e-05
 norm_eps = 1e-06
 logit_temp = 0.1
+
+
+def scan_the_pairs_all(shard_in, where_dim):
+    shard_in = jnp.moveaxis(shard_in, 0, where_dim)
+    t_next = shard_in.shape
+    return shard_in.reshape(
+        *t_next[:where_dim], t_next[where_dim] * t_next[where_dim + 1], *t_next[where_dim + 2 :]
+    )
 
 
 def extended(block, sides, width):
@@ -131,7 +139,23 @@
         tiled=True,
     ).astype(jnp.bfloat16)
     own_targets = make_targets(code_choice, codebook, quant_weight)
-    all_targets = lax.all_gather(own_targets, "seq", axis=1, tiled=True)
+    axis_len = jax.lax.axis_size("seq")
+    found = [(c, (c + 1) % axis_len) for c in range(axis_len)]
+    xs_all = [(s, pp) for pp, s in found]
+    vec_out, z1 = ([], [])
+    for m in range(axis_len - 1):
+        if m % 2 == 0:
+            vec_out.append(
+                jax.lax.ppermute(
+                    vec_out[-1] if vec_out else own_targets, axis_name="seq", perm=found
+                )
+            )
+        else:
+            z1.append(jax.lax.ppermute(z1[-1] if z1 else own_targets, "seq", perm=xs_all))
+    carry = jnp.stack([*vec_out[::-1], own_targets, *z1], 0)
+    shaped = jax.lax.axis_index("seq") - len(vec_out)
+    carry = carry[(jnp.arange(axis_len) - shaped) % axis_len]
+    all_targets = scan_the_pairs_all(carry, 1)
     is_masked = lax.dynamic_slice_in_dim(masked, lax.axis_index("tensor") * utt_rows, utt_rows, 0)
     return jax.vmap(utterance_loss)(context, own_targets, all_targets, negative_ids, is_masked)
 

time: 514 us -> 535 us (1.041)
  starting transfers between devices: 7.3 us -> 40.1 us
  waiting for transfers between devices: 149 us -> 118 us
  local copies, waits for them, and re-layouts: 267 us -> 285 us
    all_gather x1 -> x0, waiting for transfers between devices: 41.1 us -> none  [on_device(): all_targets = lax.all_gather(own_targets, 'seq', axis=1, tiled=True)]
    ppermute x0 -> x15, starting transfers between devices: none -> 32.8 us  [the longest x7 21.1 us: on_device(): jax.lax.ppermute(z1[-1] if z1 else own_targets, 'seq', perm=xs_all)]
    unnamed x14 -> x35, local copies, waits for them, and re-layouts: 1.32 us -> 14.9 us
    ppermute x0 -> x15, waiting for transfers between devices: none -> 10.3 us  [the longest x8 9.19 us: on_device(): jax.lax.ppermute(vec_out[-1] if vec_out else own_targets, axis_name='seq'...]
  transfers between devices with their start and end apart: 6 -> 20, of which waited for: 6 -> 18; matrix products, arithmetic and copies ran while one was open for 2% -> 5% of each run, Pallas kernels for 0% -> 0%
where the time goes in v1:
time: 535 us; the launch traced here: 524 us
  local copies, waits for them, and re-layouts  285 us (53%)
  waiting for transfers between devices  118 us (22%)
  matrix products  43.7 us (8%)
  starting transfers between devices  40.1 us (7%)
  other arithmetic  22.2 us (4%)
  between operations  15.2 us (3%)
    dynamic_slice x16, local copies, waits for them, and re-layouts, add_block(): taps = lax.dynamic_slice_in_dim(tap_block, base, joined_taps, 0)  59.7 us
    concatenate x8, local copies, waits for them, and re-layouts, add_block(): joined = jnp.concatenate(slabs, axis=-1)  57.4 us
    gather x4, local copies, waits for them, and re-layouts, utterance_loss(): neg_dot = jnp.take_along_axis(scores, neg_ids, axis=1)  48.7 us
    psum x1, waiting for transfers between devices, on_device(): summed = lax.psum(conv_term, 'tensor')  48.5 us
    reshape x8, local copies, waits for them, and re-layouts, add_block(): jnp.transpose(taps, (1, 0, 2, 3))  36.8 us
    gather x3, local copies, waits for them, and re-layouts, utterance_loss(): neg_norm = tgt_norm[neg_ids]  35.2 us
    while x8, matrix products  30.7 us
    all_gather x1, waiting for transfers between devices, on_device(): lax.all_gather(pos_weight, ('dp', 'seq'), axis=0, tiled=True)  28.3 us
  transfers between devices with their start and end apart: 20, of which 18 were waited for; matrix products, arithmetic and copies ran while one was open for 5% of the time, Pallas kernels for 0%

profile of v1, /device:TPU:1, one launch (start us, length us, event | category | flops | bytes accessed | tf_op | source)
XLA Modules:
  0.0 524.3 jit_solution(12221575184140428047)
XLA Ops:
  12.7 48.5 %all-reduce.2.cloned.1.call-done = f32[4,64,512]{2,1,0:T(8,128)} async-done(((f32[4,64,512]{2,1,0:T(8,128)}), f32[4,64,512]{2,1,0:T(8,128)}) %all-reduce.2.cloned.1.call-update) | async-done | bytes 524304 | tf_op jit(solution)/shard_map/psum | solution.py:107
  64.9 5.1 collective-permute-start
  72.1 6.6 %collective-permute-done = bf16[4,64,480]{2,1,0:T(8,128)(2,1)S(1)} collective-permute-done((bf16[4,64,480]{2,1,0:T(8,128)(2,1)S(1)}, bf16[4,64,480]{2,1,0:T(8,128)(2,1)S(1)}, u32[]{:S(2)}, u32[]{:S(2)}) %collective-permute-start) | collective-permute-done | bytes 245792 | tf_op jit(solution)/shard_map/ppermute | solution.py:26
  78.7 4.2 collective-permute-done.1
  86.7 28.3 %all-gather.2.cloned.1.call-done = bf16[128,4,120,120]{3,2,1,0:T(8,128)(2,1)} async-done(((bf16[2,4,120,120]{3,2,1,0:T(8,128)(2,1)}), bf16[128,4,120,120]{3,2,1,0:T(8,128)(2,1)}) %all-gather.2.cloned.1.call-update) | async-done | bytes 14745616 | tf_op jit(solution)/shard_map/all_gather | solution.py:128
  114.9 222.8 %while.16 = (s32[]{:T(128)}, f32[4,64,4,120]{3,1,0,2:T(8,128)}, bf16[128,4,120,120]{3,2,1,0:T(8,128)(2,1)}, bf16[4,192,4,120]{3,1,0,2:T(8,128)(2,1)S(1)}, s32[]{...) while((s32[]{:T(128)}, f32[4,64,4,120]{3,1,0,2:T(8,128)}, ...), condition=%wide.region_5.6_spmd.clone, body=%wide.region_4.5_spmd.clone.sunk | while | flops 472105024 | bytes 34530440 | solution.py:83
  117.9 7.2 %concatenate.26 = bf16[4,64,4,1920]{3,1,0,2:T(8,128)(2,1)} concatenate(bf16[4,64,4,120]{3,1,0,2:T(8,128)(2,1)} %get-tuple-element.238, bf16[4,64,4,120]{3,1,0,2:T(8,128)(2,1)} %get-tuple-element.239, bf16[4,64,4,120]{3,1,0,2:T(8,128)(2,1)} %get-tuple-element.240, bf16[4,64,4,120]{3,1,0,2:T(8,128)(2,1)} %get-tuple-element.241, bf16[4,64,4,120]{3,1,0,2:T(8,128)(2,1)} %get-tuple-element.242, ...), dimensions={3} | concatenate | bytes 7864320 | tf_op jit(solution)/shard_map/while/body/eval_jaxpr/concatenate | solution.py:76
  128.1 4.4 copy.47
  132.5 4.6 reshape.374
  137.1 3.8 fusion.190
  144.8 7.2 %concatenate.26 = bf16[4,64,4,1920]{3,1,0,2:T(8,128)(2,1)} concatenate(bf16[4,64,4,120]{3,1,0,2:T(8,128)(2,1)} %get-tuple-element.238, bf16[4,64,4,120]{3,1,0,2:T(8,128)(2,1)} %get-tuple-element.239, bf16[4,64,4,120]{3,1,0,2:T(8,128)(2,1)} %get-tuple-element.240, bf16[4,64,4,120]{3,1,0,2:T(8,128)(2,1)} %get-tuple-element.241, bf16[4,64,4,120]{3,1,0,2:T(8,128)(2,1)} %get-tuple-element.242, ...), dimensions={3} | concatenate | bytes 7864320 | tf_op jit(solution)/shard_map/while/body/eval_jaxpr/concatenate | solution.py:76
  155.0 4.4 copy.47
  159.5 4.6 reshape.374
  164.1 3.8 fusion.190
  172.8 7.2 %concatenate.26 = bf16[4,64,4,1920]{3,1,0,2:T(8,128)(2,1)} concatenate(bf16[4,64,4,120]{3,1,0,2:T(8,128)(2,1)} %get-tuple-element.238, bf16[4,64,4,120]{3,1,0,2:T(8,128)(2,1)} %get-tuple-element.239, bf16[4,64,4,120]{3,1,0,2:T(8,128)(2,1)} %get-tuple-element.240, bf16[4,64,4,120]{3,1,0,2:T(8,128)(2,1)} %get-tuple-element.241, bf16[4,64,4,120]{3,1,0,2:T(8,128)(2,1)} %get-tuple-element.242, ...), dimensions={3} | concatenate | bytes 7864320 | tf_op jit(solution)/shard_map/while/body/eval_jaxpr/concatenate | solution.py:76
  183.0 4.4 copy.47
  187.5 4.6 reshape.374
  192.1 3.8 fusion.190
  200.8 7.2 %concatenate.26 = bf16[4,64,4,1920]{3,1,0,2:T(8,128)(2,1)} concatenate(bf16[4,64,4,120]{3,1,0,2:T(8,128)(2,1)} %get-tuple-element.238, bf16[4,64,4,120]{3,1,0,2:T(8,128)(2,1)} %get-tuple-element.239, bf16[4,64,4,120]{3,1,0,2:T(8,128)(2,1)} %get-tuple-element.240, bf16[4,64,4,120]{3,1,0,2:T(8,128)(2,1)} %get-tuple-element.241, bf16[4,64,4,120]{3,1,0,2:T(8,128)(2,1)} %get-tuple-element.242, ...), dimensions={3} | concatenate | bytes 7864320 | tf_op jit(solution)/shard_map/while/body/eval_jaxpr/concatenate | solution.py:76
  211.0 4.4 copy.47
  215.5 4.6 reshape.374
  220.1 3.8 fusion.190
  228.8 7.2 %concatenate.26 = bf16[4,64,4,1920]{3,1,0,2:T(8,128)(2,1)} concatenate(bf16[4,64,4,120]{3,1,0,2:T(8,128)(2,1)} %get-tuple-element.238, bf16[4,64,4,120]{3,1,0,2:T(8,128)(2,1)} %get-tuple-element.239, bf16[4,64,4,120]{3,1,0,2:T(8,128)(2,1)} %get-tuple-element.240, bf16[4,64,4,120]{3,1,0,2:T(8,128)(2,1)} %get-tuple-element.241, bf16[4,64,4,120]{3,1,0,2:T(8,128)(2,1)} %get-tuple-element.242, ...), dimensions={3} | concatenate | bytes 7864320 | tf_op jit(solution)/shard_map/while/body/eval_jaxpr/concatenate | solution.py:76
  239.0 4.4 copy.47
  243.4 4.6 reshape.374
  248.0 3.8 fusion.190
  256.8 7.2 %concatenate.26 = bf16[4,64,4,1920]{3,1,0,2:T(8,128)(2,1)} concatenate(bf16[4,64,4,120]{3,1,0,2:T(8,128)(2,1)} %get-tuple-element.238, bf16[4,64,4,120]{3,1,0,2:T(8,128)(2,1)} %get-tuple-element.239, bf16[4,64,4,120]{3,1,0,2:T(8,128)(2,1)} %get-tuple-element.240, bf16[4,64,4,120]{3,1,0,2:T(8,128)(2,1)} %get-tuple-element.241, bf16[4,64,4,120]{3,1,0,2:T(8,128)(2,1)} %get-tuple-element.242, ...), dimensions={3} | concatenate | bytes 7864320 | tf_op jit(solution)/shard_map/while/body/eval_jaxpr/concatenate | solution.py:76
  267.0 4.4 copy.47
  271.4 4.6 reshape.374
  276.0 3.8 fusion.190
  284.7 7.2 %concatenate.26 = bf16[4,64,4,1920]{3,1,0,2:T(8,128)(2,1)} concatenate(bf16[4,64,4,120]{3,1,0,2:T(8,128)(2,1)} %get-tuple-element.238, bf16[4,64,4,120]{3,1,0,2:T(8,128)(2,1)} %get-tuple-element.239, bf16[4,64,4,120]{3,1,0,2:T(8,128)(2,1)} %get-tuple-element.240, bf16[4,64,4,120]{3,1,0,2:T(8,128)(2,1)} %get-tuple-element.241, bf16[4,64,4,120]{3,1,0,2:T(8,128)(2,1)} %get-tuple-element.242, ...), dimensions={3} | concatenate | bytes 7864320 | tf_op jit(solution)/shard_map/while/body/eval_jaxpr/concatenate | solution.py:76
  295.0 4.4 copy.47
  299.4 4.6 reshape.374
  304.0 3.8 fusion.190
  312.7 7.2 %concatenate.26 = bf16[4,64,4,1920]{3,1,0,2:T(8,128)(2,1)} concatenate(bf16[4,64,4,120]{3,1,0,2:T(8,128)(2,1)} %get-tuple-element.238, bf16[4,64,4,120]{3,1,0,2:T(8,128)(2,1)} %get-tuple-element.239, bf16[4,64,4,120]{3,1,0,2:T(8,128)(2,1)} %get-tuple-element.240, bf16[4,64,4,120]{3,1,0,2:T(8,128)(2,1)} %get-tuple-element.241, bf16[4,64,4,120]{3,1,0,2:T(8,128)(2,1)} %get-tuple-element.242, ...), dimensions={3} | concatenate | bytes 7864320 | tf_op jit(solution)/shard_map/while/body/eval_jaxpr/concatenate | solution.py:76
  323.0 4.4 copy.47
  327.4 4.6 reshape.374
  332.0 3.8 fusion.190
  340.9 3.8 fusion.4
  347.1 19.2 %reduce-scatter.2.cloned.1.call-done = f32[1,64,1024]{2,1,0:T(8,128)} async-done(((f32[4,64,1024]{2,1,0:T(8,128)}), f32[1,64,1024]{2,1,0:T(8,128)}) %reduce-scatter.2.cloned.1.call-update) | async-done | bytes 262160 | tf_op jit(solution)/shard_map/reduce_scatter | solution.py:135
  368.0 3.6 collective-permute-start.2
  389.4 3.5 collective-permute-start.13
  393.9 4.7 collective-permute-start.14
  400.0 4.7 collective-permute-start.15
  406.0 4.6 collective-permute-start.16
  425.7 3.6 gather_fusion
  432.3 48.5 %gather_fusion.1 = f32[6400]{0:T(1024)S(1)} fusion(f32[1,64,1024]{2,1,0:T(8,128)S(1)} %convolution_bitcast_fusion, s32[6400]{0:T(1024)S(1)} %reshape.336), kind=kCustom, calls=%fused_computation.1 | custom fusion | bytes 128000 | tf_op jit(solution)/shard_map/vmap(jit(take_along_axis))/gather | solution.py:55
  480.9 35.1 %gather_fusion.2 = f32[6400]{0:T(1024)S(1)} fusion(f32[1,1024]{1,0:T(1,128)S(1)} %bitcast.120, s32[6400]{0:T(1024)S(1)} %reshape.344), kind=kCustom, calls=%fused_computation.2 | custom fusion | bytes 102400 | tf_op jit(solution)/shard_map/vmap()/gather | solution.py:56
  (130 shorter events, 124.6 us)
Async XLA Ops:
  7.4 359.0 %copy-start = (bf16[1024,1024]{1,0:T(8,128)(2,1)S(1)}, bf16[1024,1024]{1,0:T(8,128)(2,1)}, u32[]{:S(2)}) copy-start(bf16[1024,1024]{1,0:T(8,128)(2,1)} %param.20) | copy-start | bytes 6291460
  7.4 55.1 %copy-start.7 = (bf16[512,480]{0,1:T(8,128)(2,1)S(1)}, bf16[512,480]{0,1:T(8,128)(2,1)}, u32[]{:S(2)}) copy-start(bf16[512,480]{0,1:T(8,128)(2,1)} %param.15) | copy-start | bytes 1474564
  7.4 55.1 %copy-start.8 = (bf16[480]{0:T(512)(128)(2,1)S(1)}, bf16[480]{0:T(512)(128)(2,1)}, u32[]{:S(2)}) copy-start(bf16[480]{0:T(512)(128)(2,1)} %param.16) | copy-start | bytes 2884
  7.4 53.9 %all-reduce.2.cloned.1.call-start = ((), (), s32[]{:S(2)}) async-start(), calls=%async_computation.1 | async-start | bytes 1048576 | tf_op jit(solution)/shard_map/psum | solution.py:107
  10.5 104.4 %all-gather.2.cloned.1.call-start = ((), (), s32[]{:S(2)}) async-start(), calls=%async_computation.2 | async-start | bytes 15974400 | tf_op jit(solution)/shard_map/all_gather | solution.py:128
  11.1 355.3 %reduce-scatter.2.cloned.1.call-start = ((), (), s32[]{:S(2)}) async-start(), calls=%async_computation.3 | async-start | bytes 1310720 | tf_op jit(solution)/shard_map/reduce_scatter | solution.py:135
  64.9 21.7 %copy-start.3 = (bf16[4,64,480]{2,1,0:T(8,128)(2,1)}, bf16[4,64,480]{2,1,0:T(8,128)(2,1)S(1)}, u32[]{:S(2)}) copy-start(bf16[4,64,480]{2,1,0:T(8,128)(2,1)S(1)} %fusion.1) | copy-start | bytes 737284
  64.9 13.8 %collective-permute-start = (bf16[4,64,480]{2,1,0:T(8,128)(2,1)S(1)}, bf16[4,64,480]{2,1,0:T(8,128)(2,1)S(1)}, u32[]{:S(2)}, u32[]{:S(2)}) collective-permute-start(bf16[4,64,480]{2,1,0:T(8,128)(2,1)S(1)} %fusion.1), channel_id=1, source_target_pairs={{0,4},{4,8},{8,12},{12,16},{16,20},{20,24},{24,28},{28,32},{32,36}... | collective-permute-start | bytes 737288 | tf_op jit(solution)/shard_map/ppermute | solution.py:26
  70.0 12.9 %collective-permute-start.1 = (bf16[4,64,480]{2,1,0:T(8,128)(2,1)S(1)}, bf16[4,64,480]{2,1,0:T(8,128)(2,1)}, u32[]{:S(2)}, u32[]{:S(2)}) collective-permute-start(bf16[4,64,480]{2,1,0:T(8,128)(2,1)S(1)} %fusion.1), channel_id=1, source_target_pairs={{4,0},{8,4},{12,8},{16,12},{20,16},{24,20},{28,24},{32,28},{36,32}... | collective-permute-start | bytes 737288 | tf_op jit(solution)/shard_map/ppermute | solution.py:29
  338.9 2.0 copy-start.4
  340.9 3.8 copy-start.6
  344.7 35.7 %copy-start.5 = (s32[1,64,100]{2,1,0:T(8,128)S(1)}, s32[1,64,100]{2,1,0:T(8,128)}, u32[]{:S(2)}) copy-start(s32[1,64,100]{2,1,0:T(8,128)} %param.23) | copy-start | bytes 76804
  368.0 5.5 %collective-permute-start.2 = (bf16[1,64,1024]{2,1,0:T(8,128)(2,1)S(1)}, bf16[1,64,1024]{2,1,0:T(8,128)(2,1)S(1)}, u32[]{:S(2)}, u32[]{:S(2)}) collective-permute-start(bf16[1,64,1024]{2,1,0:T(8,128)(2,1)S(1)} %bitcast.125), channel_id=1, source_target_pairs={{0,4},{4,8},{8,12},{12,16},{16,20},{20,24},{24,28},{28,32},{32,36}... | collective-permute-start | bytes 393224 | tf_op jit(solution)/shard_map/ppermute | solution.py:149
  373.5 4.4 collective-permute-start.3
  375.9 4.7 collective-permute-start.10
  377.9 4.6 collective-permute-start.4
  380.6 4.4 collective-permute-start.11
  382.5 5.6 %collective-permute-start.5 = (bf16[1,64,1024]{2,1,0:T(8,128)(2,1)S(1)}, bf16[1,64,1024]{2,1,0:T(8,128)(2,1)S(1)}, u32[]{:S(2)}, u32[]{:S(2)}) collective-permute-start(bf16[1,64,1024]{2,1,0:T(8,128)(2,1)S(1)} %collective-permute-done.4), channel_id=1, source_target_pairs={{0,4},{4,8},{8,12},{12,16},{16,20},{20,24},{24,28},{28,32},{32,36}... | collective-permute-start | bytes 393224 | tf_op jit(solution)/shard_map/ppermute | solution.py:149
  385.0 4.4 collective-permute-start.12
  388.1 5.7 %collective-permute-start.6 = (bf16[1,64,1024]{2,1,0:T(8,128)(2,1)S(1)}, bf16[1,64,1024]{2,1,0:T(8,128)(2,1)}, u32[]{:S(2)}, u32[]{:S(2)}) collective-permute-start(bf16[1,64,1024]{2,1,0:T(8,128)(2,1)S(1)} %collective-permute-done.5), channel_id=1, source_target_pairs={{0,4},{4,8},{8,12},{12,16},{16,20},{20,24},{24,28},{28,32},{32,36}... | collective-permute-start | bytes 393224 | tf_op jit(solution)/shard_map/ppermute | solution.py:149
  389.4 4.5 collective-permute-start.13
  393.9 5.9 %collective-permute-start.7 = (bf16[1,64,1024]{2,1,0:T(8,128)(2,1)}, bf16[1,64,1024]{2,1,0:T(8,128)(2,1)}, u32[]{:S(2)}, u32[]{:S(2)}) collective-permute-start(bf16[1,64,1024]{2,1,0:T(8,128)(2,1)} %collective-permute-done.6), channel_id=1, source_target_pairs={{0,4},{4,8},{8,12},{12,16},{16,20},{20,24},{24,28},{28,32},{32,36}... | collective-permute-start | bytes 393224 | tf_op jit(solution)/shard_map/ppermute | solution.py:149
  393.9 6.1 %collective-permute-start.14 = (bf16[1,64,1024]{2,1,0:T(8,128)(2,1)S(1)}, bf16[1,64,1024]{2,1,0:T(8,128)(2,1)}, u32[]{:S(2)}, u32[]{:S(2)}) collective-permute-start(bf16[1,64,1024]{2,1,0:T(8,128)(2,1)S(1)} %collective-permute-done.13), channel_id=1, source_target_pairs={{4,0},{8,4},{12,8},{16,12},{20,16},{24,20},{28,24},{32,28},{36,32}... | collective-permute-start | bytes 393224 | tf_op jit(solution)/shard_map/ppermute | solution.py:154
  399.8 5.9 %collective-permute-start.8 = (bf16[1,64,1024]{2,1,0:T(8,128)(2,1)}, bf16[1,64,1024]{2,1,0:T(8,128)(2,1)}, u32[]{:S(2)}, u32[]{:S(2)}) collective-permute-start(bf16[1,64,1024]{2,1,0:T(8,128)(2,1)} %collective-permute-done.7), channel_id=1, source_target_pairs={{0,4},{4,8},{8,12},{12,16},{16,20},{20,24},{24,28},{28,32},{32,36}... | collective-permute-start | bytes 393224 | tf_op jit(solution)/shard_map/ppermute | solution.py:149
  400.0 5.9 %collective-permute-start.15 = (bf16[1,64,1024]{2,1,0:T(8,128)(2,1)}, bf16[1,64,1024]{2,1,0:T(8,128)(2,1)S(1)}, u32[]{:S(2)}, u32[]{:S(2)}) collective-permute-start(bf16[1,64,1024]{2,1,0:T(8,128)(2,1)} %collective-permute-done.14), channel_id=1, source_target_pairs={{4,0},{8,4},{12,8},{16,12},{20,16},{24,20},{28,24},{32,28},{36,32}... | collective-permute-start | bytes 393224 | tf_op jit(solution)/shard_map/ppermute | solution.py:154
  405.7 5.8 %collective-permute-start.9 = (bf16[1,64,1024]{2,1,0:T(8,128)(2,1)}, bf16[1,64,1024]{2,1,0:T(8,128)(2,1)S(1)}, u32[]{:S(2)}, u32[]{:S(2)}) collective-permute-start(bf16[1,64,1024]{2,1,0:T(8,128)(2,1)} %collective-permute-done.8), channel_id=1, source_target_pairs={{0,4},{4,8},{8,12},{12,16},{16,20},{20,24},{24,28},{28,32},{32,36}... | collective-permute-start | bytes 393224 | tf_op jit(solution)/shard_map/ppermute | solution.py:149
  406.0 19.1 %collective-permute-start.16 = (bf16[1,64,1024]{2,1,0:T(8,128)(2,1)S(1)}, bf16[1,64,1024]{2,1,0:T(8,128)(2,1)S(1)}, u32[]{:S(2)}, u32[]{:S(2)}) collective-permute-start(bf16[1,64,1024]{2,1,0:T(8,128)(2,1)S(1)} %collective-permute-done.15), channel_id=1, source_target_pairs={{4,0},{8,4},{12,8},{16,12},{20,16},{24,20},{28,24},{32,28},{36,32}... | collective-permute-start | bytes 393224 | tf_op jit(solution)/shard_map/ppermute | solution.py:154
  425.7 5.9 %copy-start.2 = (f32[1,64,1024]{2,1,0:T(8,128)S(1)}, f32[1,64,1024]{2,1,0:T(8,128)}, u32[]{:S(2)}) copy-start(f32[1,64,1024]{2,1,0:T(8,128)} %reduce-scatter.2.cloned.1.call-done) | copy-start | bytes 786436
  429.3 2.2 copy-start.1
Sparse Core Ops, SparseCore 0:
  10.6 50.5 all-reduce.1
  344.8 21.5 reduce-scatter.1
Sparse Core Ops, SparseCore 1:
  13.7 101.2 all-gather.1
